TPU v7x, 256 devices: a whole 4x4x8 slice. The times are simulated.
256 devices in a mesh: rows: 16 (over x, y_lo, core), cols: 16 (over z, y_hi).
Axes of the slice: x: 4, y: 4 (y_hi: 2, y_lo: 2; y = y_hi * 2 + y_lo), z: 8, core: 2. Of those that a mesh axis runs over, the one named last changes fastest.
Arguments:
- unary: float32 [21, 256, 2048], P(None, 'rows', 'cols'), may hold values from -8 to 300
- features: bfloat16 [64, 256, 2048], P(None, 'rows', 'cols'), may hold values from -9 to 9
- compat: float32 [21, 21], replicated, may hold values from -6 to 6
- grad_output: float32 [21, 256, 2048], P(None, 'rows', 'cols'), may hold values from -6 to 6
Outputs:
- unary_grad: float32 [21, 256, 2048], P(None, 'rows', 'cols')
- feature_grad: float32 [64, 256, 2048], P(None, 'rows', 'cols')
- compat_grad: float32 [21, 21], replicated
All inputs are finite; a program needn't handle non-finite values.
Results may differ from a plain program's by a relative error of at most 0.0003.
Values may be sent and summed in bfloat16 or wider, within the bound.
A program may use at most 128 MiB of HBM per device.

v0:
```python
import math
import jax
import jax.numpy as jnp
from jax import lax
from jax.sharding import PartitionSpec as P

ITERS = 2
THETA_PIXELS = 3.0
WINDOW_OFFSETS = [
    (row_step, col_step)
    for row_step in range(-3, 4)
    for col_step in range(-3, 4)
    if row_step != 0 or col_step != 0
]


def with_halo(block, sides, width):
    for axis, dim in sides:
        count = lax.axis_size(axis)
        forward = [(i, i + 1) for i in range(count - 1)]
        backward = [(target, source) for source, target in forward]
        low = lax.ppermute(
            lax.slice_in_dim(block, block.shape[dim] - width, None, axis=dim), axis, forward
        )
        high = lax.ppermute(lax.slice_in_dim(block, 0, width, axis=dim), axis, backward)
        block = jnp.concatenate([low, block, high], axis=dim)
    return block


def spatial_weight(row_step, col_step):
    return math.exp(
        -(row_step * row_step + col_step * col_step) / (2.0 * THETA_PIXELS * THETA_PIXELS)
    )


def shifted_view(padded, row_step, col_step, height, width_cells):
    return padded[
        :, 3 + row_step : 3 + row_step + height, 3 + col_step : 3 + col_step + width_cells
    ]


def affinity(padded_features):
    height = padded_features.shape[1] - 6
    width_cells = padded_features.shape[2] - 6
    center = shifted_view(padded_features, 0, 0, height, width_cells).astype(jnp.float32)
    factor = 1.0 / (2.0 * padded_features.shape[0])
    layers = []
    for row_step, col_step in WINDOW_OFFSETS:
        shifted = shifted_view(padded_features, row_step, col_step, height, width_cells).astype(
            jnp.float32
        )
        distance = jnp.sum((shifted - center) * (shifted - center), axis=0)
        layers.append(spatial_weight(row_step, col_step) * jnp.exp(-distance * factor))
    return jnp.stack(layers)


def message(kernel, padded):
    height = kernel.shape[1]
    width_cells = kernel.shape[2]
    total = jnp.zeros((padded.shape[0], height, width_cells), jnp.float32)
    for number, (row_step, col_step) in enumerate(WINDOW_OFFSETS):
        total = total + kernel[number][None] * shifted_view(
            padded, row_step, col_step, height, width_cells
        )
    return total


def pair_terms(grad_padded, prob_padded):
    height = grad_padded.shape[1] - 6
    width_cells = grad_padded.shape[2] - 6
    grad_center = shifted_view(grad_padded, 0, 0, height, width_cells)
    prob_center = shifted_view(prob_padded, 0, 0, height, width_cells)
    layers = []
    for row_step, col_step in WINDOW_OFFSETS:
        prob_shift = shifted_view(prob_padded, row_step, col_step, height, width_cells)
        grad_shift = shifted_view(grad_padded, row_step, col_step, height, width_cells)
        layers.append(jnp.sum(grad_center * prob_shift + grad_shift * prob_center, axis=0))
    return jnp.stack(layers)


def feature_term(coefs, kernel, padded_features):
    height = kernel.shape[1]
    width_cells = kernel.shape[2]
    center = shifted_view(padded_features, 0, 0, height, width_cells).astype(jnp.float32)
    factor = 1.0 / padded_features.shape[0]
    total = jnp.zeros(center.shape, jnp.float32)
    for number, (row_step, col_step) in enumerate(WINDOW_OFFSETS):
        shifted = shifted_view(padded_features, row_step, col_step, height, width_cells).astype(
            jnp.float32
        )
        weight_map = coefs[number] * kernel[number] * factor
        total = total + weight_map[None] * (shifted - center)
    return total


def mix(compat, values):
    return jnp.einsum("cd,dhw->chw", compat, values, precision=lax.Precision.HIGHEST)


def mix_back(compat, values):
    return jnp.einsum("cd,chw->dhw", compat, values, precision=lax.Precision.HIGHEST)


def outer_sum(left, right):
    return jnp.einsum("chw,dhw->cd", left, right, precision=lax.Precision.HIGHEST)


def softmax_grad(prob, cotangent):
    return prob * (cotangent - jnp.sum(cotangent * prob, axis=0, keepdims=True))


def on_device(unary, features, compat, grad_output):
    height = unary.shape[1]
    width_cells = unary.shape[2]
    total_pixels = height * lax.axis_size("rows") * width_cells * lax.axis_size("cols")
    reach = 0
    feat_wide = with_halo(features, (("rows", 1), ("cols", 2)), 3)
    cotangent = grad_output
    start_prob = jax.nn.softmax(unary, axis=0)
    kern_store = affinity(feat_wide)

    def kernel_at():
        return kern_store

    prob_list = [start_prob]
    pad_list = [reach]
    wide_list = []
    message_list = []
    for step in range(ITERS):
        current = prob_list[-1]
        prob_wide = with_halo(current, (("rows", 1), ("cols", 2)), 3)
        wide_pad = 3
        wide_list.append((prob_wide, wide_pad))
        out_pad = wide_pad - 3
        message_out = message(kernel_at(), prob_wide)
        message_list.append(message_out)
        logits = unary - mix(compat, message_out)
        next_prob = jax.nn.softmax(logits, axis=0)
        prob_list.append(next_prob)
        pad_list.append(out_pad)
    unary_sum = jnp.zeros(unary.shape, jnp.float32)
    compat_sum = jnp.zeros(compat.shape, jnp.float32)
    coefs = jnp.zeros((len(WINDOW_OFFSETS), height, width_cells), jnp.float32)
    for step in reversed(range(ITERS)):
        later_prob = prob_list[step + 1]
        logit_grad = softmax_grad(later_prob, cotangent)
        unary_sum = unary_sum + logit_grad
        compat_sum = compat_sum - outer_sum(logit_grad, message_list[step])
        msg_grad = -mix_back(compat, logit_grad)
        grad_wide = with_halo(msg_grad, (("rows", 1), ("cols", 2)), 3)
        cotangent = message(kernel_at(), grad_wide)
        prob_wide, wide_pad = wide_list[step]
        coefs = coefs + pair_terms(grad_wide, prob_wide)
    unary_grad = unary_sum + softmax_grad(prob_list[0], cotangent)
    feature_grad = feature_term(coefs, kernel_at(), feat_wide)
    compat_grad = lax.psum(compat_sum, ("rows", "cols")) / math.sqrt(total_pixels)
    return (unary_grad, feature_grad, compat_grad)


def solution(mesh):
    placed = (P(None, "rows", "cols"), P(None, "rows", "cols"), P(), P(None, "rows", "cols"))
    return jax.shard_map(
        on_device,
        mesh=mesh,
        in_specs=placed,
        out_specs=(P(None, "rows", "cols"), P(None, "rows", "cols"), P()),
        check_vma=False,
    )
```

profile of v0, /device:TPU:33, one launch (start us, length us, event | category | flops | bytes accessed | tf_op | source)
XLA Modules:
  0.0 314.2 jit_solution(16345287022579159694)
XLA Ops:
  3.7 3.8 %collective-permute-start.3 = (f32[21,3,128]{2,0,1:T(8,128)S(1)}, f32[21,3,128]{2,0,1:T(8,128)S(1)}, u32[]{:S(2)}, u32[]{:S(2)}) collective-permute-start(f32[21,3,128]{2,0,1:T(8,128)S(1)} %get-tuple-element.238), channel_id=1, source_target_pairs={{0,16},{16,32},{32,48},{48,64},{64,80},{80,96},{96,112},{112,128},... | collective-permute-start | bytes 96776 | tf_op jit(solution)/shard_map/ppermute | solution.py:22
  9.5 3.6 %collective-permute-start = (bf16[64,3,128]{2,1,0:T(4,128)(2,1)S(1)}, bf16[64,3,128]{2,1,0:T(4,128)(2,1)S(1)}, u32[]{:S(2)}, u32[]{:S(2)}) collective-permute-start(bf16[64,3,128]{2,1,0:T(4,128)(2,1)S(1)} %get-tuple-element.229), channel_id=1, source_target_pairs={{0,16},{16,32},{32,48},{48,64},{64,80},{80,96},{96,112},{112,128},... | collective-permute-start | bytes 147464 | tf_op jit(solution)/shard_map/ppermute | solution.py:22
  15.2 4.5 %collective-permute-start.5 = (f32[21,22,3]{2,0,1:T(8,128)S(1)}, f32[21,22,3]{2,0,1:T(8,128)S(1)}, u32[]{:S(2)}, u32[]{:S(2)}) collective-permute-start(f32[21,22,3]{2,0,1:T(8,128)S(1)} %get-tuple-element.227), channel_id=1, source_target_pairs={{0,1},{1,2},{2,3},{3,4},{4,5},{5,6},{6,7},{7,8},{8,9},{9,10},{10,1... | collective-permute-start | bytes 16640 | tf_op jit(solution)/shard_map/ppermute | solution.py:22
  19.8 3.2 %collective-permute-start.7 = (f32[21,22,3]{2,0,1:T(8,128)S(1)}, f32[21,22,3]{2,0,1:T(8,128)S(1)}, u32[]{:S(2)}, u32[]{:S(2)}) collective-permute-start(f32[21,22,3]{2,0,1:T(8,128)S(1)} %get-tuple-element.228), channel_id=1, source_target_pairs={{1,0},{2,1},{3,2},{4,3},{5,4},{6,5},{7,6},{8,7},{9,8},{10,9},{11,1... | collective-permute-start | bytes 16640 | tf_op jit(solution)/shard_map/ppermute | solution.py:25
  23.0 8.2 %collective-permute-done.5 = f32[21,22,3]{2,0,1:T(8,128)S(1)} collective-permute-done((f32[21,22,3]{2,0,1:T(8,128)S(1)}, f32[21,22,3]{2,0,1:T(8,128)S(1)}, u32[]{:S(2)}, u32[]{:S(2)}) %collective-permute-start.5) | collective-permute-done | bytes 5576 | tf_op jit(solution)/shard_map/ppermute | solution.py:22
  36.7 3.8 %collective-permute-start.2 = (bf16[64,22,3]{2,1,0:T(8,128)(2,1)S(1)}, bf16[64,22,3]{2,1,0:T(8,128)(2,1)S(1)}, u32[]{:S(2)}, u32[]{:S(2)}) collective-permute-start(bf16[64,22,3]{2,1,0:T(8,128)(2,1)S(1)} %get-tuple-element.212), channel_id=1, source_target_pairs={{0,1},{1,2},{2,3},{3,4},{4,5},{5,6},{6,7},{7,8},{8,9},{9,10},{10,1... | collective-permute-start | bytes 25352 | tf_op jit(solution)/shard_map/ppermute | solution.py:22
  40.5 15.3 %collective-permute-done.6 = bf16[64,22,3]{2,1,0:T(8,128)(2,1)S(1)} collective-permute-done((bf16[64,22,3]{2,1,0:T(8,128)(2,1)S(1)}, bf16[64,22,3]{2,1,0:T(8,128)(2,1)S(1)}, u32[]{:S(2)}, u32[]{:S(2)}) %collective-permute-start.6) | collective-permute-done | bytes 8480 | tf_op jit(solution)/shard_map/ppermute | solution.py:25
  83.4 5.8 %collective-permute-start.8 = (f32[21,3,128]{2,0,1:T(8,128)S(1)}, f32[21,3,128]{2,0,1:T(8,128)S(1)}, u32[]{:S(2)}, u32[]{:S(2)}) collective-permute-start(f32[21,3,128]{2,0,1:T(8,128)S(1)} %get-tuple-element.236), channel_id=1, source_target_pairs={{0,16},{16,32},{32,48},{48,64},{64,80},{80,96},{96,112},{112,128},... | collective-permute-start | bytes 96776 | tf_op jit(solution)/shard_map/ppermute | solution.py:22
  91.1 3.3 %collective-permute-done.9 = f32[21,3,128]{2,0,1:T(8,128)S(1)} collective-permute-done((f32[21,3,128]{2,0,1:T(8,128)S(1)}, f32[21,3,128]{2,0,1:T(8,128)S(1)}, u32[]{:S(2)}, u32[]{:S(2)}) %collective-permute-start.9) | collective-permute-done | bytes 32288 | tf_op jit(solution)/shard_map/ppermute | solution.py:25
  94.6 4.8 %collective-permute-start.10 = (f32[21,22,3]{2,0,1:T(8,128)S(1)}, f32[21,22,3]{2,0,1:T(8,128)S(1)}, u32[]{:S(2)}, u32[]{:S(2)}) collective-permute-start(f32[21,22,3]{2,0,1:T(8,128)S(1)} %get-tuple-element.223), channel_id=1, source_target_pairs={{0,1},{1,2},{2,3},{3,4},{4,5},{5,6},{6,7},{7,8},{8,9},{9,10},{10,1... | collective-permute-start | bytes 16640 | tf_op jit(solution)/shard_map/ppermute | solution.py:22
  102.5 7.3 %collective-permute-done.10 = f32[21,22,3]{2,0,1:T(8,128)S(1)} collective-permute-done((f32[21,22,3]{2,0,1:T(8,128)S(1)}, f32[21,22,3]{2,0,1:T(8,128)S(1)}, u32[]{:S(2)}, u32[]{:S(2)}) %collective-permute-start.10) | collective-permute-done | bytes 5576 | tf_op jit(solution)/shard_map/ppermute | solution.py:22
  118.5 4.6 %collective-permute-start.12 = (f32[21,3,128]{2,0,1:T(8,128)S(1)}, f32[21,3,128]{2,0,1:T(8,128)S(1)}, u32[]{:S(2)}, u32[]{:S(2)}) collective-permute-start(f32[21,3,128]{2,0,1:T(8,128)S(1)} %get-tuple-element.234), channel_id=1, source_target_pairs={{0,16},{16,32},{32,48},{48,64},{64,80},{80,96},{96,112},{112,128},... | collective-permute-start | bytes 96776 | tf_op jit(solution)/shard_map/ppermute | solution.py:22
  125.0 3.3 %collective-permute-done.13 = f32[21,3,128]{2,0,1:T(8,128)S(1)} collective-permute-done((f32[21,3,128]{2,0,1:T(8,128)S(1)}, f32[21,3,128]{2,0,1:T(8,128)S(1)}, u32[]{:S(2)}, u32[]{:S(2)}) %collective-permute-start.13) | collective-permute-done | bytes 32288 | tf_op jit(solution)/shard_map/ppermute | solution.py:25
  128.5 3.9 %collective-permute-start.14 = (f32[21,22,3]{2,0,1:T(8,128)S(1)}, f32[21,22,3]{2,0,1:T(8,128)S(1)}, u32[]{:S(2)}, u32[]{:S(2)}) collective-permute-start(f32[21,22,3]{2,0,1:T(8,128)S(1)} %get-tuple-element.219), channel_id=1, source_target_pairs={{0,1},{1,2},{2,3},{3,4},{4,5},{5,6},{6,7},{7,8},{8,9},{9,10},{10,1... | collective-permute-start | bytes 16640 | tf_op jit(solution)/shard_map/ppermute | solution.py:22
  132.4 3.8 %collective-permute-start.15 = (f32[21,22,3]{2,0,1:T(8,128)S(1)}, f32[21,22,3]{2,0,1:T(8,128)S(1)}, u32[]{:S(2)}, u32[]{:S(2)}) collective-permute-start(f32[21,22,3]{2,0,1:T(8,128)S(1)} %get-tuple-element.220), channel_id=1, source_target_pairs={{1,0},{2,1},{3,2},{4,3},{5,4},{6,5},{7,6},{8,7},{9,8},{10,9},{11,1... | collective-permute-start | bytes 16640 | tf_op jit(solution)/shard_map/ppermute | solution.py:25
  136.9 5.8 %collective-permute-done.14 = f32[21,22,3]{2,0,1:T(8,128)S(1)} collective-permute-done((f32[21,22,3]{2,0,1:T(8,128)S(1)}, f32[21,22,3]{2,0,1:T(8,128)S(1)}, u32[]{:S(2)}, u32[]{:S(2)}) %collective-permute-start.14) | collective-permute-done | bytes 5576 | tf_op jit(solution)/shard_map/ppermute | solution.py:22
  152.1 4.4 %add_reduce_fusion.48 = (f32[16,128]{1,0:T(8,128)}, f32[16,128]{1,0:T(8,128)}, f32[16,128]{1,0:T(8,128)}, f32[16,128]{1,0:T(8,128)}, f32[16,128]{1,0:T(8,128)}, ...) fusion(f32[21,16,128]{2,0,1:T(8,128)S(1)} %fusion.11, ...), kind=kLoop, calls=%fused_computation.349 | loop fusion | flops 5830656 | bytes 9657344 | tf_op jit(solution)/shard_map/reduce_sum | solution.py:77
  159.8 81.1 %psum.7 = f32[21,21]{1,0:T(8,128)S(1)} all-reduce(f32[21,21]{1,0:T(8,128)S(1)} %fusion.15), channel_id=1, replica_groups=mesh['rows'=16,'cols'=16] {'rows','cols'}, use_global_device_ids=true, to_apply=%region_153.0 | all-reduce | flops 441 | bytes 3528 | tf_op jit(solution)/shard_map/psum | solution.py:156
  257.8 3.8 %collective-permute-start.18 = (f32[21,22,3]{2,0,1:T(8,128)S(1)}, f32[21,22,3]{2,0,1:T(8,128)S(1)}, u32[]{:S(2)}, u32[]{:S(2)}) collective-permute-start(f32[21,22,3]{2,0,1:T(8,128)S(1)} %get-tuple-element.215), channel_id=1, source_target_pairs={{0,1},{1,2},{2,3},{3,4},{4,5},{5,6},{6,7},{7,8},{8,9},{9,10},{10,1... | collective-permute-start | bytes 16640 | tf_op jit(solution)/shard_map/ppermute | solution.py:22
  261.6 4.1 %collective-permute-start.19 = (f32[21,22,3]{2,0,1:T(8,128)S(1)}, f32[21,22,3]{2,0,1:T(8,128)S(1)}, u32[]{:S(2)}, u32[]{:S(2)}) collective-permute-start(f32[21,22,3]{2,0,1:T(8,128)S(1)} %get-tuple-element.216), channel_id=1, source_target_pairs={{1,0},{2,1},{3,2},{4,3},{5,4},{6,5},{7,6},{8,7},{9,8},{10,9},{11,1... | collective-permute-start | bytes 16640 | tf_op jit(solution)/shard_map/ppermute | solution.py:25
  266.0 6.7 %collective-permute-done.18 = f32[21,22,3]{2,0,1:T(8,128)S(1)} collective-permute-done((f32[21,22,3]{2,0,1:T(8,128)S(1)}, f32[21,22,3]{2,0,1:T(8,128)S(1)}, u32[]{:S(2)}, u32[]{:S(2)}) %collective-permute-start.18) | collective-permute-done | bytes 5576 | tf_op jit(solution)/shard_map/ppermute | solution.py:22
  272.7 3.5 %collective-permute-done.19 = f32[21,22,3]{2,0,1:T(8,128)S(1)} collective-permute-done((f32[21,22,3]{2,0,1:T(8,128)S(1)}, f32[21,22,3]{2,0,1:T(8,128)S(1)}, u32[]{:S(2)}, u32[]{:S(2)}) %collective-permute-start.19) | collective-permute-done | bytes 5576 | tf_op jit(solution)/shard_map/ppermute | solution.py:25
  290.9 13.9 %fusion.7 = f32[21,16,128]{2,0,1:T(8,128)S(1)} fusion(f32[21,16,128]{2,0,1:T(8,128)S(1)} %copy-done.10, f32[16,128]{1,0:T(8,128)} %fusion.19, f32[21,16,128]{2,1,0:T(8,128)} %param.7, f32[21,16,128]{2,0,1:T(8,128)} %copy-done.11, f32[16,128]{1,0:T(8,128)} %get-tuple-element.242, f32[16,128]{1,0:T(8,128)S(1)} %copy-done.13, f32[16,128]{1,0:T(8,128)S(1)} %reduce_max.27, ...), kind=kOutput, calls=%fused_computation.55 | output fusion | flops 9205780 | bytes 18972672 | tf_op jit(solution)/shard_map/sub | solution.py:109
  305.9 8.3 %multiply_add_fusion = f32[64,16,128]{2,1,0:T(8,128)} fusion(bf16[64,16,128]{2,1,0:T(8,128)(2,1)S(1)} %copy-done.6, bf16[64,3,128]{2,1,0:T(4,128)(2,1)S(1)} %collective-permute-done, f32[16,128]{1,0:T(8,128)} %get-tuple-element.162, f32[16,128]{1,0:T(8,128)} %get-tuple-element.163, f32[16,128]{1,0:T(8,128)} %get-tuple-element.164, ...), kind=kLoop, calls=%fused_computation.80 | loop fusion | flops 26345472 | bytes 13025280 | tf_op jit(solution)/shard_map/add | solution.py:92
  (516 shorter events, 99.3 us)
Async XLA Ops:
  3.7 11.4 %collective-permute-start.3 = (f32[21,3,128]{2,0,1:T(8,128)S(1)}, f32[21,3,128]{2,0,1:T(8,128)S(1)}, u32[]{:S(2)}, u32[]{:S(2)}) collective-permute-start(f32[21,3,128]{2,0,1:T(8,128)S(1)} %get-tuple-element.238), channel_id=1, source_target_pairs={{0,16},{16,32},{32,48},{48,64},{64,80},{80,96},{96,112},{112,128},... | collective-permute-start | bytes 96776 | tf_op jit(solution)/shard_map/ppermute | solution.py:22
  7.5 7.6 %collective-permute-start.4 = (f32[21,3,128]{2,0,1:T(8,128)S(1)}, f32[21,3,128]{2,0,1:T(8,128)S(1)}, u32[]{:S(2)}, u32[]{:S(2)}) collective-permute-start(f32[21,3,128]{2,0,1:T(8,128)S(1)} %get-tuple-element.239), channel_id=1, source_target_pairs={{16,0},{32,16},{48,32},{64,48},{80,64},{96,80},{112,96},{128,112},... | collective-permute-start | bytes 96776 | tf_op jit(solution)/shard_map/ppermute | solution.py:25
  9.5 23.8 %collective-permute-start = (bf16[64,3,128]{2,1,0:T(4,128)(2,1)S(1)}, bf16[64,3,128]{2,1,0:T(4,128)(2,1)S(1)}, u32[]{:S(2)}, u32[]{:S(2)}) collective-permute-start(bf16[64,3,128]{2,1,0:T(4,128)(2,1)S(1)} %get-tuple-element.229), channel_id=1, source_target_pairs={{0,16},{16,32},{32,48},{48,64},{64,80},{80,96},{96,112},{112,128},... | collective-permute-start | bytes 147464 | tf_op jit(solution)/shard_map/ppermute | solution.py:22
  13.1 20.1 %collective-permute-start.1 = (bf16[64,3,128]{2,1,0:T(4,128)(2,1)S(1)}, bf16[64,3,128]{2,1,0:T(4,128)(2,1)S(1)}, u32[]{:S(2)}, u32[]{:S(2)}) collective-permute-start(bf16[64,3,128]{2,1,0:T(4,128)(2,1)S(1)} %get-tuple-element.230), channel_id=1, source_target_pairs={{16,0},{32,16},{48,32},{64,48},{80,64},{96,80},{112,96},{128,112},... | collective-permute-start | bytes 147464 | tf_op jit(solution)/shard_map/ppermute | solution.py:25
  15.2 15.9 %collective-permute-start.5 = (f32[21,22,3]{2,0,1:T(8,128)S(1)}, f32[21,22,3]{2,0,1:T(8,128)S(1)}, u32[]{:S(2)}, u32[]{:S(2)}) collective-permute-start(f32[21,22,3]{2,0,1:T(8,128)S(1)} %get-tuple-element.227), channel_id=1, source_target_pairs={{0,1},{1,2},{2,3},{3,4},{4,5},{5,6},{6,7},{7,8},{8,9},{9,10},{10,1... | collective-permute-start | bytes 16640 | tf_op jit(solution)/shard_map/ppermute | solution.py:22
  19.8 13.3 %collective-permute-start.7 = (f32[21,22,3]{2,0,1:T(8,128)S(1)}, f32[21,22,3]{2,0,1:T(8,128)S(1)}, u32[]{:S(2)}, u32[]{:S(2)}) collective-permute-start(f32[21,22,3]{2,0,1:T(8,128)S(1)} %get-tuple-element.228), channel_id=1, source_target_pairs={{1,0},{2,1},{3,2},{4,3},{5,4},{6,5},{7,6},{8,7},{9,8},{10,9},{11,1... | collective-permute-start | bytes 16640 | tf_op jit(solution)/shard_map/ppermute | solution.py:25
  33.7 22.1 %collective-permute-start.6 = (bf16[64,22,3]{2,1,0:T(8,128)(2,1)S(1)}, bf16[64,22,3]{2,1,0:T(8,128)(2,1)S(1)}, u32[]{:S(2)}, u32[]{:S(2)}) collective-permute-start(bf16[64,22,3]{2,1,0:T(8,128)(2,1)S(1)} %get-tuple-element.211), channel_id=1, source_target_pairs={{1,0},{2,1},{3,2},{4,3},{5,4},{6,5},{7,6},{8,7},{9,8},{10,9},{11,1... | collective-permute-start | bytes 25352 | tf_op jit(solution)/shard_map/ppermute | solution.py:25
  36.7 19.1 %collective-permute-start.2 = (bf16[64,22,3]{2,1,0:T(8,128)(2,1)S(1)}, bf16[64,22,3]{2,1,0:T(8,128)(2,1)S(1)}, u32[]{:S(2)}, u32[]{:S(2)}) collective-permute-start(bf16[64,22,3]{2,1,0:T(8,128)(2,1)S(1)} %get-tuple-element.212), channel_id=1, source_target_pairs={{0,1},{1,2},{2,3},{3,4},{4,5},{5,6},{6,7},{7,8},{8,9},{9,10},{10,1... | collective-permute-start | bytes 25352 | tf_op jit(solution)/shard_map/ppermute | solution.py:22
  83.4 7.7 %collective-permute-start.8 = (f32[21,3,128]{2,0,1:T(8,128)S(1)}, f32[21,3,128]{2,0,1:T(8,128)S(1)}, u32[]{:S(2)}, u32[]{:S(2)}) collective-permute-start(f32[21,3,128]{2,0,1:T(8,128)S(1)} %get-tuple-element.236), channel_id=1, source_target_pairs={{0,16},{16,32},{32,48},{48,64},{64,80},{80,96},{96,112},{112,128},... | collective-permute-start | bytes 96776 | tf_op jit(solution)/shard_map/ppermute | solution.py:22
  89.2 5.3 %collective-permute-start.9 = (f32[21,3,128]{2,0,1:T(8,128)S(1)}, f32[21,3,128]{2,0,1:T(8,128)S(1)}, u32[]{:S(2)}, u32[]{:S(2)}) collective-permute-start(f32[21,3,128]{2,0,1:T(8,128)S(1)} %get-tuple-element.237), channel_id=1, source_target_pairs={{16,0},{32,16},{48,32},{64,48},{80,64},{96,80},{112,96},{128,112},... | collective-permute-start | bytes 96776 | tf_op jit(solution)/shard_map/ppermute | solution.py:25
  94.6 15.2 %collective-permute-start.10 = (f32[21,22,3]{2,0,1:T(8,128)S(1)}, f32[21,22,3]{2,0,1:T(8,128)S(1)}, u32[]{:S(2)}, u32[]{:S(2)}) collective-permute-start(f32[21,22,3]{2,0,1:T(8,128)S(1)} %get-tuple-element.223), channel_id=1, source_target_pairs={{0,1},{1,2},{2,3},{3,4},{4,5},{5,6},{6,7},{7,8},{8,9},{9,10},{10,1... | collective-permute-start | bytes 16640 | tf_op jit(solution)/shard_map/ppermute | solution.py:22
  99.4 12.0 %collective-permute-start.11 = (f32[21,22,3]{2,0,1:T(8,128)S(1)}, f32[21,22,3]{2,0,1:T(8,128)S(1)}, u32[]{:S(2)}, u32[]{:S(2)}) collective-permute-start(f32[21,22,3]{2,0,1:T(8,128)S(1)} %get-tuple-element.224), channel_id=1, source_target_pairs={{1,0},{2,1},{3,2},{4,3},{5,4},{6,5},{7,6},{8,7},{9,8},{10,9},{11,1... | collective-permute-start | bytes 16640 | tf_op jit(solution)/shard_map/ppermute | solution.py:25
  118.5 6.5 %collective-permute-start.12 = (f32[21,3,128]{2,0,1:T(8,128)S(1)}, f32[21,3,128]{2,0,1:T(8,128)S(1)}, u32[]{:S(2)}, u32[]{:S(2)}) collective-permute-start(f32[21,3,128]{2,0,1:T(8,128)S(1)} %get-tuple-element.234), channel_id=1, source_target_pairs={{0,16},{16,32},{32,48},{48,64},{64,80},{80,96},{96,112},{112,128},... | collective-permute-start | bytes 96776 | tf_op jit(solution)/shard_map/ppermute | solution.py:22
  123.0 5.3 %collective-permute-start.13 = (f32[21,3,128]{2,0,1:T(8,128)S(1)}, f32[21,3,128]{2,0,1:T(8,128)S(1)}, u32[]{:S(2)}, u32[]{:S(2)}) collective-permute-start(f32[21,3,128]{2,0,1:T(8,128)S(1)} %get-tuple-element.235), channel_id=1, source_target_pairs={{16,0},{32,16},{48,32},{64,48},{80,64},{96,80},{112,96},{128,112},... | collective-permute-start | bytes 96776 | tf_op jit(solution)/shard_map/ppermute | solution.py:25
  128.5 14.3 %collective-permute-start.14 = (f32[21,22,3]{2,0,1:T(8,128)S(1)}, f32[21,22,3]{2,0,1:T(8,128)S(1)}, u32[]{:S(2)}, u32[]{:S(2)}) collective-permute-start(f32[21,22,3]{2,0,1:T(8,128)S(1)} %get-tuple-element.219), channel_id=1, source_target_pairs={{0,1},{1,2},{2,3},{3,4},{4,5},{5,6},{6,7},{7,8},{8,9},{9,10},{10,1... | collective-permute-start | bytes 16640 | tf_op jit(solution)/shard_map/ppermute | solution.py:22
  132.4 12.9 %collective-permute-start.15 = (f32[21,22,3]{2,0,1:T(8,128)S(1)}, f32[21,22,3]{2,0,1:T(8,128)S(1)}, u32[]{:S(2)}, u32[]{:S(2)}) collective-permute-start(f32[21,22,3]{2,0,1:T(8,128)S(1)} %get-tuple-element.220), channel_id=1, source_target_pairs={{1,0},{2,1},{3,2},{4,3},{5,4},{6,5},{7,6},{8,7},{9,8},{10,9},{11,1... | collective-permute-start | bytes 16640 | tf_op jit(solution)/shard_map/ppermute | solution.py:25
  158.6 98.9 %copy-start.125 = (f32[16,128]{1,0:T(8,128)S(1)}, f32[16,128]{1,0:T(8,128)}, u32[]{:S(2)}) copy-start(f32[16,128]{1,0:T(8,128)} %get-tuple-element.14) | copy-start | bytes 24580
  158.7 98.9 %copy-start.130 = (f32[16,128]{1,0:T(8,128)S(1)}, f32[16,128]{1,0:T(8,128)}, u32[]{:S(2)}) copy-start(f32[16,128]{1,0:T(8,128)} %get-tuple-element.8) | copy-start | bytes 24580
  158.7 98.9 %copy-start.129 = (f32[16,128]{1,0:T(8,128)S(1)}, f32[16,128]{1,0:T(8,128)}, u32[]{:S(2)}) copy-start(f32[16,128]{1,0:T(8,128)} %get-tuple-element.7) | copy-start | bytes 24580
  158.7 98.9 %copy-start.128 = (f32[16,128]{1,0:T(8,128)S(1)}, f32[16,128]{1,0:T(8,128)}, u32[]{:S(2)}) copy-start(f32[16,128]{1,0:T(8,128)} %get-tuple-element.6) | copy-start | bytes 24580
  241.5 16.1 %collective-permute-start.16 = (f32[21,3,128]{2,0,1:T(8,128)S(1)}, f32[21,3,128]{2,0,1:T(8,128)S(1)}, u32[]{:S(2)}, u32[]{:S(2)}) collective-permute-start(f32[21,3,128]{2,0,1:T(8,128)S(1)} %get-tuple-element.232), channel_id=1, source_target_pairs={{0,16},{16,32},{32,48},{48,64},{64,80},{80,96},{96,112},{112,128},... | collective-permute-start | bytes 96776 | tf_op jit(solution)/shard_map/ppermute | solution.py:22
  243.5 14.2 %collective-permute-start.17 = (f32[21,3,128]{2,0,1:T(8,128)S(1)}, f32[21,3,128]{2,0,1:T(8,128)S(1)}, u32[]{:S(2)}, u32[]{:S(2)}) collective-permute-start(f32[21,3,128]{2,0,1:T(8,128)S(1)} %get-tuple-element.233), channel_id=1, source_target_pairs={{16,0},{32,16},{48,32},{64,48},{80,64},{96,80},{112,96},{128,112},... | collective-permute-start | bytes 96776 | tf_op jit(solution)/shard_map/ppermute | solution.py:25
  257.8 14.9 %collective-permute-start.18 = (f32[21,22,3]{2,0,1:T(8,128)S(1)}, f32[21,22,3]{2,0,1:T(8,128)S(1)}, u32[]{:S(2)}, u32[]{:S(2)}) collective-permute-start(f32[21,22,3]{2,0,1:T(8,128)S(1)} %get-tuple-element.215), channel_id=1, source_target_pairs={{0,1},{1,2},{2,3},{3,4},{4,5},{5,6},{6,7},{7,8},{8,9},{9,10},{10,1... | collective-permute-start | bytes 16640 | tf_op jit(solution)/shard_map/ppermute | solution.py:22
  261.6 14.6 %collective-permute-start.19 = (f32[21,22,3]{2,0,1:T(8,128)S(1)}, f32[21,22,3]{2,0,1:T(8,128)S(1)}, u32[]{:S(2)}, u32[]{:S(2)}) collective-permute-start(f32[21,22,3]{2,0,1:T(8,128)S(1)} %get-tuple-element.216), channel_id=1, source_target_pairs={{1,0},{2,1},{3,2},{4,3},{5,4},{6,5},{7,6},{8,7},{9,8},{10,9},{11,1... | collective-permute-start | bytes 16640 | tf_op jit(solution)/shard_map/ppermute | solution.py:25
  (152 other events, 6748.9 us)
where the time goes:
time: 319 us; the launch traced here: 314 us
  other arithmetic  84.1 us (26%)
  blocking collectives  81.1 us (25%)
  starting transfers between devices  67.7 us (21%)
  waiting for transfers between devices  59.5 us (19%)
  local copies, waits for them, and re-layouts  14.4 us (5%)
  between operations  3.99 us (1%)
  matrix products  3.54 us (1%)
    psum x1, blocking collectives, on_device(): lax.psum(compat_sum, ('rows', 'cols')) / math.sqrt(total_pixels)  81.1 us
    ppermute x10, starting transfers between devices, with_halo(): lax.ppermute(lax.slice_in_dim(block, block.shape[dim] - width, None, axis...  40.5 us
    ppermute x10, waiting for transfers between devices, with_halo(): lax.ppermute(lax.slice_in_dim(block, 0, width, axis=dim), axis, backward)  31.4 us
    ppermute x10, waiting for transfers between devices, with_halo(): lax.ppermute(lax.slice_in_dim(block, block.shape[dim] - width, None, axis...  28.1 us
    ppermute x10, starting transfers between devices, with_halo(): lax.ppermute(lax.slice_in_dim(block, 0, width, axis=dim), axis, backward)  27.2 us
    reduce_sum x16, other arithmetic, pair_terms(): jnp.sum(grad_center * prob_shift + grad_shift * prob_center, axis=0)  16.8 us
    mul x24, other arithmetic, affinity(): spatial_weight(row_step, col_step) * jnp.exp(-distance * factor)  14 us
    sub x1, other arithmetic, softmax_grad(): return prob * (cotangent - jnp.sum(cotangent * prob, axis=0, keepdims=True))  13.9 us
  transfers between devices with their start and end apart: 20, of which 11 were waited for; matrix products, arithmetic and copies ran while one was open for 4% of the time, Pallas kernels for 0%

commit v1 on v0

--- a/solution.py
+++ b/solution.py
@@ -3,6 +3,7 @@
 import jax.numpy as jnp
 from jax import lax
 from jax.sharding import PartitionSpec as P
+from jax.lax import all_gather
 
 ITERS = 2
 THETA_PIXELS = 3.0
@@ -153,7 +154,8 @@
         coefs = coefs + pair_terms(grad_wide, prob_wide)
     unary_grad = unary_sum + softmax_grad(prob_list[0], cotangent)
     feature_grad = feature_term(coefs, kernel_at(), feat_wide)
-    compat_grad = lax.psum(compat_sum, ("rows", "cols")) / math.sqrt(total_pixels)
+    get_cube = lambda named_axis, slab_in: jnp.sum(all_gather(slab_in, named_axis), axis=0)
+    compat_grad = get_cube(("rows", "cols"), compat_sum) / math.sqrt(total_pixels)
     return (unary_grad, feature_grad, compat_grad)
 
 

time: 319 us -> 948 us (2.97)
  the two profiles are of different devices: /device:TPU:33 before, /device:TPU:16 now
where the time goes in v1:
time: 948 us; the launch traced here: 944 us
  blocking collectives  677 us (71%)
  other arithmetic  88.1 us (9%)
  starting transfers between devices  60.6 us (6%)
  waiting for transfers between devices  60 us (6%)
  local copies, waits for them, and re-layouts  50.7 us (5%)
    all_gather x1, blocking collectives, on_device(): all_gather(slab_in, named_axis)  677 us
    unnamed x340, local copies, waits for them, and re-layouts  48.3 us
    ppermute x10, starting transfers between devices, with_halo(): lax.ppermute(lax.slice_in_dim(block, block.shape[dim] - width, None, axis...  38.3 us
    ppermute x10, waiting for transfers between devices, with_halo(): lax.ppermute(lax.slice_in_dim(block, 0, width, axis=dim), axis, backward)  32.3 us
    ppermute x10, waiting for transfers between devices, with_halo(): lax.ppermute(lax.slice_in_dim(block, block.shape[dim] - width, None, axis...  27.7 us
    ppermute x10, starting transfers between devices, with_halo(): lax.ppermute(lax.slice_in_dim(block, 0, width, axis=dim), axis, backward)  22.3 us
  transfers between devices with their start and end apart: 20, of which 11 were waited for; matrix products, arithmetic and copies ran while one was open for 5% of the time, Pallas kernels for 0%

profile of v1, /device:TPU:16, one launch (start us, length us, event | category | flops | bytes accessed | tf_op | source)
XLA Modules:
  0.0 943.5 jit_solution(16974011498606952358)
XLA Ops:
  7.8 4.1 collective-permute-start
  13.4 3.9 collective-permute-start.5
  17.3 3.5 collective-permute-start.7
  20.8 11.1 %collective-permute-done.5 = f32[21,22,3]{2,0,1:T(8,128)S(1)} collective-permute-done((f32[21,22,3]{2,0,1:T(8,128)S(1)}, f32[21,22,3]{2,0,1:T(8,128)S(1)}, u32[]{:S(2)}, u32[]{:S(2)}) %collective-permute-start.5) | collective-permute-done | bytes 5576 | tf_op jit(solution)/shard_map/ppermute | solution.py:23
  34.5 6.3 collective-permute-start.2
  40.8 7.7 collective-permute-done.6
  48.5 8.3 collective-permute-done.2
  87.8 4.9 collective-permute-done.9
  92.8 3.6 collective-permute-start.10
  96.4 3.9 collective-permute-start.11
  100.3 3.4 collective-permute-done.10
  103.8 4.9 collective-permute-done.11
  115.9 4.3 collective-permute-start.12
  121.5 4.1 collective-permute-done.13
  125.8 4.5 collective-permute-start.14
  136.8 5.9 collective-permute-done.15
  149.5 4.5 add_reduce_fusion.48
  156.9 3.4 collective-permute-start.16
  162.3 677.2 %all-gather.1 = f32[256,21,21]{2,1,0:T(8,128)} all-gather(f32[1,21,21]{2,1,0:T(8,128)S(1)} %fusion.16), channel_id=2, replica_groups=mesh['rows'=16,'cols'=16] {'rows','cols'}, dimensions={0}, use_global_device_ids=true | all-gather | bytes 453348 | tf_op jit(solution)/shard_map/all_gather | solution.py:157
  888.4 4.3 collective-permute-start.18
  892.7 3.7 collective-permute-start.19
  898.7 4.8 collective-permute-done.19
  918.5 14.6 %fusion.7 = f32[21,16,128]{2,0,1:T(8,128)} fusion(f32[21,16,128]{2,0,1:T(8,128)S(1)} %copy-done.10, f32[16,128]{1,0:T(8,128)} %fusion.20, f32[21,16,128]{2,1,0:T(8,128)} %param.7, f32[21,16,128]{2,0,1:T(8,128)} %copy-done.11, f32[16,128]{1,0:T(8,128)} %get-tuple-element.245, f32[16,128]{1,0:T(8,128)S(1)} %copy-done.14, f32[16,128]{1,0:T(8,128)S(1)} %reduce_max.27, ...), kind=kOutput, calls=%fused_computation.55 | output fusion | flops 9205780 | bytes 18972672 | tf_op jit(solution)/shard_map/sub | solution.py:110
  934.7 8.6 multiply_add_fusion
  (449 shorter events, 134.5 us)
Async XLA Ops:
  0.6 82.8 %copy-start = (f32[21,21]{1,0:T(8,128)S(1)}, f32[21,21]{1,0:T(8,128)}, u32[]{:S(2)}) copy-start(f32[21,21]{1,0:T(8,128)} %param.6) | copy-start | bytes 5296
  3.7 9.5 %collective-permute-start.3 = (f32[21,3,128]{2,0,1:T(8,128)S(1)}, f32[21,3,128]{2,0,1:T(8,128)S(1)}, u32[]{:S(2)}, u32[]{:S(2)}) collective-permute-start(f32[21,3,128]{2,0,1:T(8,128)S(1)} %get-tuple-element.241), channel_id=1, source_target_pairs={{0,16},{16,32},{32,48},{48,64},{64,80},{80,96},{96,112},{112,128},... | collective-permute-start | bytes 96776 | tf_op jit(solution)/shard_map/ppermute | solution.py:23
  5.4 7.8 collective-permute-start.4
  7.8 24.3 %collective-permute-start = (bf16[64,3,128]{2,1,0:T(4,128)(2,1)S(1)}, bf16[64,3,128]{2,1,0:T(4,128)(2,1)S(1)}, u32[]{:S(2)}, u32[]{:S(2)}) collective-permute-start(bf16[64,3,128]{2,1,0:T(4,128)(2,1)S(1)} %get-tuple-element.232), channel_id=1, source_target_pairs={{0,16},{16,32},{32,48},{48,64},{64,80},{80,96},{96,112},{112,128},... | collective-permute-start | bytes 147464 | tf_op jit(solution)/shard_map/ppermute | solution.py:23
  11.9 20.2 %collective-permute-start.1 = (bf16[64,3,128]{2,1,0:T(4,128)(2,1)S(1)}, bf16[64,3,128]{2,1,0:T(4,128)(2,1)S(1)}, u32[]{:S(2)}, u32[]{:S(2)}) collective-permute-start(bf16[64,3,128]{2,1,0:T(4,128)(2,1)S(1)} %get-tuple-element.233), channel_id=1, source_target_pairs={{16,0},{32,16},{48,32},{64,48},{80,64},{96,80},{112,96},{128,112},... | collective-permute-start | bytes 147464 | tf_op jit(solution)/shard_map/ppermute | solution.py:26
  13.4 18.5 %collective-permute-start.5 = (f32[21,22,3]{2,0,1:T(8,128)S(1)}, f32[21,22,3]{2,0,1:T(8,128)S(1)}, u32[]{:S(2)}, u32[]{:S(2)}) collective-permute-start(f32[21,22,3]{2,0,1:T(8,128)S(1)} %get-tuple-element.230), channel_id=1, source_target_pairs={{0,1},{1,2},{2,3},{3,4},{4,5},{5,6},{6,7},{7,8},{8,9},{9,10},{10,1... | collective-permute-start | bytes 16640 | tf_op jit(solution)/shard_map/ppermute | solution.py:23
  17.3 14.6 %collective-permute-start.7 = (f32[21,22,3]{2,0,1:T(8,128)S(1)}, f32[21,22,3]{2,0,1:T(8,128)S(1)}, u32[]{:S(2)}, u32[]{:S(2)}) collective-permute-start(f32[21,22,3]{2,0,1:T(8,128)S(1)} %get-tuple-element.231), channel_id=1, source_target_pairs={{1,0},{2,1},{3,2},{4,3},{5,4},{6,5},{7,6},{8,7},{9,8},{10,9},{11,1... | collective-permute-start | bytes 16640 | tf_op jit(solution)/shard_map/ppermute | solution.py:26
  32.5 16.0 %collective-permute-start.6 = (bf16[64,22,3]{2,1,0:T(8,128)(2,1)S(1)}, bf16[64,22,3]{2,1,0:T(8,128)(2,1)S(1)}, u32[]{:S(2)}, u32[]{:S(2)}) collective-permute-start(bf16[64,22,3]{2,1,0:T(8,128)(2,1)S(1)} %get-tuple-element.214), channel_id=1, source_target_pairs={{1,0},{2,1},{3,2},{4,3},{5,4},{6,5},{7,6},{8,7},{9,8},{10,9},{11,1... | collective-permute-start | bytes 25352 | tf_op jit(solution)/shard_map/ppermute | solution.py:26
  34.5 22.4 %collective-permute-start.2 = (bf16[64,22,3]{2,1,0:T(8,128)(2,1)S(1)}, bf16[64,22,3]{2,1,0:T(8,128)(2,1)S(1)}, u32[]{:S(2)}, u32[]{:S(2)}) collective-permute-start(bf16[64,22,3]{2,1,0:T(8,128)(2,1)S(1)} %get-tuple-element.215), channel_id=1, source_target_pairs={{0,1},{1,2},{2,3},{3,4},{4,5},{5,6},{6,7},{7,8},{8,9},{9,10},{10,1... | collective-permute-start | bytes 25352 | tf_op jit(solution)/shard_map/ppermute | solution.py:23
  66.7 82.4 %copy-start.21 = (f32[16,128]{1,0:T(8,128)}, f32[16,128]{1,0:T(8,128)S(1)}, u32[]{:S(2)}) copy-start(f32[16,128]{1,0:T(8,128)S(1)} %get-tuple-element.257) | copy-start | bytes 24580
  66.7 82.4 %copy-start.23 = (f32[16,128]{1,0:T(8,128)}, f32[16,128]{1,0:T(8,128)S(1)}, u32[]{:S(2)}) copy-start(f32[16,128]{1,0:T(8,128)S(1)} %get-tuple-element.258) | copy-start | bytes 24580
  67.5 81.7 %copy-start.25 = (f32[16,128]{1,0:T(8,128)}, f32[16,128]{1,0:T(8,128)S(1)}, u32[]{:S(2)}) copy-start(f32[16,128]{1,0:T(8,128)S(1)} %get-tuple-element.251) | copy-start | bytes 24580
  84.5 3.3 collective-permute-start.8
  86.4 6.2 collective-permute-start.9
  92.8 11.0 %collective-permute-start.10 = (f32[21,22,3]{2,0,1:T(8,128)S(1)}, f32[21,22,3]{2,0,1:T(8,128)S(1)}, u32[]{:S(2)}, u32[]{:S(2)}) collective-permute-start(f32[21,22,3]{2,0,1:T(8,128)S(1)} %get-tuple-element.226), channel_id=1, source_target_pairs={{0,1},{1,2},{2,3},{3,4},{4,5},{5,6},{6,7},{7,8},{8,9},{9,10},{10,1... | collective-permute-start | bytes 16640 | tf_op jit(solution)/shard_map/ppermute | solution.py:23
  96.4 12.3 %collective-permute-start.11 = (f32[21,22,3]{2,0,1:T(8,128)S(1)}, f32[21,22,3]{2,0,1:T(8,128)S(1)}, u32[]{:S(2)}, u32[]{:S(2)}) collective-permute-start(f32[21,22,3]{2,0,1:T(8,128)S(1)} %get-tuple-element.227), channel_id=1, source_target_pairs={{1,0},{2,1},{3,2},{4,3},{5,4},{6,5},{7,6},{8,7},{9,8},{10,9},{11,1... | collective-permute-start | bytes 16640 | tf_op jit(solution)/shard_map/ppermute | solution.py:26
  115.9 5.7 collective-permute-start.12
  120.2 5.4 collective-permute-start.13
  125.8 11.0 %collective-permute-start.14 = (f32[21,22,3]{2,0,1:T(8,128)S(1)}, f32[21,22,3]{2,0,1:T(8,128)S(1)}, u32[]{:S(2)}, u32[]{:S(2)}) collective-permute-start(f32[21,22,3]{2,0,1:T(8,128)S(1)} %get-tuple-element.222), channel_id=1, source_target_pairs={{0,1},{1,2},{2,3},{3,4},{4,5},{5,6},{6,7},{7,8},{8,9},{9,10},{10,1... | collective-permute-start | bytes 16640 | tf_op jit(solution)/shard_map/ppermute | solution.py:23
  130.3 12.3 %collective-permute-start.15 = (f32[21,22,3]{2,0,1:T(8,128)S(1)}, f32[21,22,3]{2,0,1:T(8,128)S(1)}, u32[]{:S(2)}, u32[]{:S(2)}) collective-permute-start(f32[21,22,3]{2,0,1:T(8,128)S(1)} %get-tuple-element.223), channel_id=1, source_target_pairs={{1,0},{2,1},{3,2},{4,3},{5,4},{6,5},{7,6},{8,7},{9,8},{10,9},{11,1... | collective-permute-start | bytes 16640 | tf_op jit(solution)/shard_map/ppermute | solution.py:26
  156.9 731.3 %collective-permute-start.16 = (f32[21,3,128]{2,0,1:T(8,128)S(1)}, f32[21,3,128]{2,0,1:T(8,128)S(1)}, u32[]{:S(2)}, u32[]{:S(2)}) collective-permute-start(f32[21,3,128]{2,0,1:T(8,128)S(1)} %get-tuple-element.235), channel_id=1, source_target_pairs={{0,16},{16,32},{32,48},{48,64},{64,80},{80,96},{96,112},{112,128},... | collective-permute-start | bytes 96776 | tf_op jit(solution)/shard_map/ppermute | solution.py:23
  160.4 727.8 %collective-permute-start.17 = (f32[21,3,128]{2,0,1:T(8,128)S(1)}, f32[21,3,128]{2,0,1:T(8,128)S(1)}, u32[]{:S(2)}, u32[]{:S(2)}) collective-permute-start(f32[21,3,128]{2,0,1:T(8,128)S(1)} %get-tuple-element.236), channel_id=1, source_target_pairs={{16,0},{32,16},{48,32},{64,48},{80,64},{96,80},{112,96},{128,112},... | collective-permute-start | bytes 96776 | tf_op jit(solution)/shard_map/ppermute | solution.py:26
  888.4 10.3 %collective-permute-start.18 = (f32[21,22,3]{2,0,1:T(8,128)S(1)}, f32[21,22,3]{2,0,1:T(8,128)S(1)}, u32[]{:S(2)}, u32[]{:S(2)}) collective-permute-start(f32[21,22,3]{2,0,1:T(8,128)S(1)} %get-tuple-element.218), channel_id=1, source_target_pairs={{0,1},{1,2},{2,3},{3,4},{4,5},{5,6},{6,7},{7,8},{8,9},{9,10},{10,1... | collective-permute-start | bytes 16640 | tf_op jit(solution)/shard_map/ppermute | solution.py:23
  892.7 10.8 %collective-permute-start.19 = (f32[21,22,3]{2,0,1:T(8,128)S(1)}, f32[21,22,3]{2,0,1:T(8,128)S(1)}, u32[]{:S(2)}, u32[]{:S(2)}) collective-permute-start(f32[21,22,3]{2,0,1:T(8,128)S(1)} %get-tuple-element.219), channel_id=1, source_target_pairs={{1,0},{2,1},{3,2},{4,3},{5,4},{6,5},{7,6},{8,7},{9,8},{10,9},{11,1... | collective-permute-start | bytes 16640 | tf_op jit(solution)/shard_map/ppermute | solution.py:26
  (118 other events, 4064.8 us)
